TPU v7x, 32 devices: a whole 2x2x4 slice. The times are simulated.
32 devices in a mesh: dp: 4 (over y, core), expert: 2 (over x), tensor: 4 (over z).
Axes of the slice: x: 2, y: 2, z: 4, core: 2. Of those that a mesh axis runs over, the one named last changes fastest.
Arguments:
- inputs: bfloat16 [1576, 768], P(('dp', 'expert')), may hold values from -6 to 6
- first_gain: float32 [768], replicated, may hold values from 0.5 to 1.5
- first_bias: float32 [768], replicated, may hold values from -2 to 2
- attention_in: bfloat16 [3, 768, 768], P(None, None, 'tensor')
- attention_out: bfloat16 [768, 768], P('tensor'), may hold values from -0.875 to 0.875
- second_gain: float32 [768], replicated, may hold values from 0.5 to 1.5
- second_bias: float32 [768], replicated, may hold values from -2 to 2
- router_weight: float32 [768, 4], replicated
- expert_in: bfloat16 [4, 768, 3072], P('expert', None, 'tensor'), may hold values from -0.21875 to 0.21875
- expert_out: bfloat16 [4, 3072, 768], P('expert', 'tensor'), may hold values from -1.75 to 1.75
- expert_ids: int32 [1576, 2], P(('dp', 'expert')), may hold values from 0 to 3, as said below
- slot_index: int32 [1576, 2], P(('dp', 'expert')), may hold values from 0 to 98, as said below
- cotangent: bfloat16 [1576, 768], P(('dp', 'expert')), may hold values from -6 to 6
Outputs:
- layer_out: float32 [1576, 768], P(('dp', 'expert'))
- input_grad: float32 [1576, 768], P(('dp', 'expert'))
- first_gain_grad: float32 [768], P(('dp', 'expert'))
- first_bias_grad: float32 [768], P(('dp', 'expert'))
- attention_in_grad: float32 [3, 768, 768], P(None, ('dp', 'expert'), 'tensor')
- attention_out_grad: float32 [768, 768], P('tensor', ('dp', 'expert'))
- second_gain_grad: float32 [768], P(('dp', 'expert'))
- second_bias_grad: float32 [768], P(('dp', 'expert'))
- router_grad: float32 [768, 4], P(('dp', 'expert'))
- expert_in_grad: float32 [4, 768, 3072], P('expert', 'dp', 'tensor')
- expert_out_grad: float32 [4, 3072, 768], P('expert', 'tensor', 'dp')
Inputs may be any that keep to these rules, and one draw needn't show every extreme that they name: `expert_ids`: the two experts of a token differ. `slot_index`: among the 197 tokens of one index of dp and expert, the choices naming one expert hold slots 0, 1, 2 and so on, all first choices before all second choices, rows in order within each; a choice ranked 98 or later holds 98 and is dropped. Some expert fills all 98 slots from every index of dp and expert.
All inputs are finite; a program needn't handle non-finite values.
Results may differ from a plain program's by a relative error of at most 0.02.
Values may be sent and summed in bfloat16 or wider, within the bound.
A program may use at most 128 MiB of HBM per device.

v0:
```python
import math
import jax
import jax.numpy as jnp
from jax import lax
from jax.sharding import PartitionSpec as P

HEAD_DIM = 64
SEQ = 197
EPS = 1e-06
GELU_C = math.sqrt(2.0 / math.pi)


def cut_along(shard, dim, devices):
    shape = shard.shape
    tiles = shard.reshape(*shape[:dim], devices, shape[dim] // devices, *shape[dim + 1 :])
    return jnp.moveaxis(tiles, dim, 0)


def sent_and_summed(shard, axis, dim):
    devices = lax.axis_size(axis)
    tiles = lax.all_to_all(cut_along(shard, dim, devices), axis, 0, 0, tiled=True)
    return jnp.sum(tiles.astype(jnp.float32), axis=0)


def sent_together(arrays, axis, dim, along):
    widths = [math.prod(a.shape[along:]) for a in arrays]
    both = jnp.concatenate(
        [a.reshape(*a.shape[:along], w) for a, w in zip(arrays, widths)], axis=along
    )
    out = sent_and_summed(both, axis, dim)
    tiles = jnp.split(out, [sum(widths[:k]) for k in range(1, len(widths))], axis=along)
    return tuple((b.reshape(*out.shape[:along], *a.shape[along:]) for a, b in zip(arrays, tiles)))


def normalize(values):
    centre = jnp.mean(values, axis=-1, keepdims=True)
    centred = values - centre
    spread = jnp.mean(centred * centred, axis=-1, keepdims=True)
    scale = lax.rsqrt(spread + EPS)
    return (centred * scale, scale)


def norm_back(grad_out, normed, scale, gain):
    scaled = grad_out * gain
    first_mean = jnp.mean(scaled, axis=-1, keepdims=True)
    second_mean = jnp.mean(scaled * normed, axis=-1, keepdims=True)
    return scale * (scaled - first_mean - normed * second_mean)


def gelu_parts(pre):
    inner = GELU_C * (pre + 0.044715 * pre * pre * pre)
    tangent = jnp.tanh(inner)
    value = 0.5 * pre * (1.0 + tangent)
    slope = 0.5 * (1.0 + tangent) + 0.5 * pre * (1.0 - tangent * tangent) * GELU_C * (
        1.0 + 3.0 * 0.044715 * pre * pre
    )
    return (value, slope)


def per_device(
    inputs,
    first_gain,
    first_bias,
    attention_in,
    attention_out,
    second_gain,
    second_bias,
    router_weight,
    expert_in,
    expert_out,
    expert_ids,
    slot_index,
    cotangent,
):
    tokens_here = inputs.shape[0]
    model_width = inputs.shape[1]
    images = tokens_here // SEQ
    local_width = attention_in.shape[2]
    local_heads = local_width // HEAD_DIM
    owners = lax.axis_size("expert")
    experts_here = expert_in.shape[0]
    experts_all = experts_here * owners
    capacity = (2 * tokens_here - 1) // experts_all
    scaling = HEAD_DIM ** (-0.5)

    def split_heads(matrix):
        return matrix.reshape(images, SEQ, local_heads, HEAD_DIM)

    x_full = inputs.astype(jnp.float32)
    normed1, scale1 = normalize(x_full)
    first = (normed1 * first_gain + first_bias).astype(jnp.bfloat16)
    project = [
        jnp.dot(first, attention_in[which], preferred_element_type=jnp.float32).astype(jnp.bfloat16)
        for which in range(3)
    ]
    query_h, keys_h, values_h = [split_heads(part) for part in project]
    scores = (
        jnp.einsum("iqhd,ikhd->ihqk", query_h, keys_h, preferred_element_type=jnp.float32) * scaling
    )
    peak = jnp.max(scores, axis=-1, keepdims=True)
    logsum = peak[..., 0] + jnp.log(jnp.sum(jnp.exp(scores - peak), axis=-1))
    weights = jnp.exp(scores - logsum[..., None]).astype(jnp.bfloat16)
    context_h = jnp.einsum(
        "ihqk,ikhd->iqhd", weights, values_h, preferred_element_type=jnp.float32
    ).astype(jnp.bfloat16)
    context = context_h.reshape(tokens_here, local_width)
    partial_attn = jnp.dot(context, attention_out, preferred_element_type=jnp.float32)
    attended = lax.psum(partial_attn, "tensor")
    resid = x_full + attended
    normed2, scale2 = normalize(resid)
    second = (normed2 * second_gain + second_bias).astype(jnp.bfloat16)
    logits = jnp.dot(second.astype(jnp.float32), router_weight, precision=lax.Precision.HIGHEST)
    route = jax.nn.softmax(logits, axis=-1)
    valid = (slot_index < capacity).astype(jnp.float32)
    choose = (expert_ids[:, :, None] == jnp.arange(experts_all, dtype=jnp.int32)).astype(
        jnp.float32
    )
    gate = jnp.sum(route[:, None, :] * choose, axis=-1) * valid
    target = jnp.where(slot_index < capacity, expert_ids * capacity + slot_index, -1)
    chosen = (target[:, :, None] == jnp.arange(experts_all * capacity, dtype=jnp.int32)).astype(
        jnp.bfloat16
    )
    placing = jnp.sum(chosen, axis=1)
    sendbuf = jnp.einsum("rq,rd->qd", placing, second, preferred_element_type=jnp.float32).astype(
        jnp.bfloat16
    )
    sendbuf = sendbuf.reshape(owners, experts_here, capacity, model_width)
    received = lax.all_to_all(sendbuf, "expert", split_axis=0, concat_axis=0, tiled=True)
    pre = jnp.einsum("skcd,kdf->skcf", received, expert_in, preferred_element_type=jnp.float32)
    value, slope = gelu_parts(pre)
    hidden = value.astype(jnp.bfloat16)
    partial_value = jnp.einsum(
        "skcf,kfd->skcd", hidden, expert_out, preferred_element_type=jnp.float32
    )
    summed = lax.psum(partial_value, "tensor")
    returned = lax.all_to_all(
        summed.astype(jnp.bfloat16), "expert", split_axis=0, concat_axis=0, tiled=True
    )
    outcome = (returned, received, hidden, slope)
    returned = outcome[0]
    received = outcome[1]
    outputs_flat = returned.reshape(experts_all * capacity, model_width)
    picked = jnp.einsum("rjq,qd->rjd", chosen, outputs_flat, preferred_element_type=jnp.float32)
    layer_out = resid + jnp.sum(gate[..., None] * picked, axis=1)
    grad_out = cotangent.astype(jnp.float32)
    gate_grad = jnp.sum(grad_out[:, None, :] * picked, axis=-1) * valid
    slot_gate = jnp.einsum(
        "rjq,rj->q", chosen.astype(jnp.float32), gate, precision=lax.Precision.HIGHEST
    )
    slotted = jnp.einsum("rq,rd->qd", placing, cotangent, preferred_element_type=jnp.float32)
    grad_send = (
        (slot_gate[:, None] * slotted)
        .astype(jnp.bfloat16)
        .reshape(owners, experts_here, capacity, model_width)
    )
    grad_recv = lax.all_to_all(grad_send, "expert", split_axis=0, concat_axis=0, tiled=True)
    hidden = outcome[2]
    slope = outcome[3]
    hidden_grad = jnp.einsum(
        "skcd,kfd->skcf", grad_recv, expert_out, preferred_element_type=jnp.float32
    )
    pre_grad = (hidden_grad * slope).astype(jnp.bfloat16)
    local_out_grad = jnp.einsum(
        "skcf,skcd->kfd", hidden, grad_recv, preferred_element_type=jnp.float32
    )
    local_in_grad = jnp.einsum(
        "skcd,skcf->kdf", received, pre_grad, preferred_element_type=jnp.float32
    )
    partial_back = jnp.einsum(
        "skcf,kdf->skcd", pre_grad, expert_in, preferred_element_type=jnp.float32
    )
    back_sum = lax.psum(partial_back.astype(jnp.bfloat16), "tensor")
    back_home = lax.all_to_all(back_sum, "expert", split_axis=0, concat_axis=0, tiled=True)
    back_rows = jnp.einsum(
        "rjq,qd->rd",
        chosen,
        back_home.reshape(experts_all * capacity, model_width),
        preferred_element_type=jnp.float32,
    )
    expert_in_grad, expert_out_grad = (
        lax.psum_scatter(
            local_in_grad.astype(jnp.bfloat16), "dp", scatter_dimension=1, tiled=True
        ).astype(jnp.float32),
        lax.psum_scatter(
            local_out_grad.astype(jnp.bfloat16), "dp", scatter_dimension=2, tiled=True
        ).astype(jnp.float32),
    )
    route_grad = jnp.sum(gate_grad[:, :, None] * choose, axis=1)
    logit_grad = route * (route_grad - jnp.sum(route * route_grad, axis=-1, keepdims=True))
    local_router = jnp.dot(
        second.astype(jnp.float32).T, logit_grad, precision=lax.Precision.HIGHEST
    )
    second_grad = back_rows + jnp.dot(logit_grad, router_weight.T, precision=lax.Precision.HIGHEST)
    local_second_gain = jnp.sum(second_grad * normed2, axis=0)
    local_second_bias = jnp.sum(second_grad, axis=0)
    resid_grad = grad_out + norm_back(second_grad, normed2, scale2, second_gain)
    resid_low = resid_grad.astype(jnp.bfloat16)
    local_attn_out = jnp.einsum("rh,rd->hd", context, resid_low, preferred_element_type=jnp.float32)
    context_grad = jnp.einsum(
        "rd,hd->rh", resid_low, attention_out, preferred_element_type=jnp.float32
    ).astype(jnp.bfloat16)
    context_g = split_heads(context_grad)
    probs = jnp.exp(scores - logsum[..., None])
    values_grad = jnp.einsum(
        "ihqk,iqhd->ikhd", weights, context_g, preferred_element_type=jnp.float32
    ).astype(jnp.bfloat16)
    probs_grad = jnp.einsum(
        "iqhd,ikhd->ihqk", context_g, values_h, preferred_element_type=jnp.float32
    )
    delta = jnp.transpose(
        jnp.sum(context_g.astype(jnp.float32) * context_h.astype(jnp.float32), axis=-1), (0, 2, 1)
    )
    score_grad = (probs * (probs_grad - delta[..., None]) * scaling).astype(jnp.bfloat16)
    query_grad = jnp.einsum(
        "ihqk,ikhd->iqhd", score_grad, keys_h, preferred_element_type=jnp.float32
    ).astype(jnp.bfloat16)
    keys_grad = jnp.einsum(
        "ihqk,iqhd->ikhd", score_grad, query_h, preferred_element_type=jnp.float32
    ).astype(jnp.bfloat16)
    grads_flat = [
        part.reshape(tokens_here, local_width) for part in (query_grad, keys_grad, values_grad)
    ]
    local_attn_in = jnp.stack(
        [
            jnp.einsum("rd,rh->dh", first, part, preferred_element_type=jnp.float32)
            for part in grads_flat
        ]
    )
    partial_first = jnp.einsum(
        "rh,dh->rd", grads_flat[0], attention_in[0], preferred_element_type=jnp.float32
    )
    partial_first = partial_first + jnp.einsum(
        "rh,dh->rd", grads_flat[1], attention_in[1], preferred_element_type=jnp.float32
    )
    partial_first = partial_first + jnp.einsum(
        "rh,dh->rd", grads_flat[2], attention_in[2], preferred_element_type=jnp.float32
    )
    first_grad = lax.psum(partial_first.astype(jnp.bfloat16), "tensor").astype(jnp.float32)
    local_first_gain = jnp.sum(first_grad * normed1, axis=0)
    local_first_bias = jnp.sum(first_grad, axis=0)
    input_grad = resid_grad + norm_back(first_grad, normed1, scale1, first_gain)
    summed_shared = (
        sent_and_summed(local_attn_in.astype(jnp.bfloat16), ("dp", "expert"), 1),
        sent_and_summed(local_attn_out.astype(jnp.bfloat16), ("dp", "expert"), 1),
        *sent_together(
            (
                local_router.astype(jnp.bfloat16),
                local_first_gain.astype(jnp.bfloat16),
                local_first_bias.astype(jnp.bfloat16),
                local_second_gain.astype(jnp.bfloat16),
                local_second_bias.astype(jnp.bfloat16),
            ),
            ("dp", "expert"),
            0,
            1,
        ),
    )
    (
        attention_in_grad,
        attention_out_grad,
        router_grad,
        first_gain_grad,
        first_bias_grad,
        second_gain_grad,
        second_bias_grad,
    ) = summed_shared
    return (
        layer_out,
        input_grad,
        first_gain_grad,
        first_bias_grad,
        attention_in_grad,
        attention_out_grad,
        second_gain_grad,
        second_bias_grad,
        router_grad,
        expert_in_grad,
        expert_out_grad,
    )


def solution(mesh):
    in_specs = (
        P(("dp", "expert"), None),
        P(),
        P(),
        P(None, None, "tensor"),
        P("tensor", None),
        P(),
        P(),
        P(),
        P("expert", None, "tensor"),
        P("expert", "tensor", None),
        P(("dp", "expert"), None),
        P(("dp", "expert"), None),
        P(("dp", "expert"), None),
    )
    out_specs = (
        P(("dp", "expert"), None),
        P(("dp", "expert"), None),
        P(("dp", "expert")),
        P(("dp", "expert")),
        P(None, ("dp", "expert"), "tensor"),
        P("tensor", ("dp", "expert")),
        P(("dp", "expert")),
        P(("dp", "expert")),
        P(("dp", "expert"), None),
        P("expert", "dp", "tensor"),
        P("expert", "tensor", "dp"),
    )
    return jax.shard_map(
        per_device, mesh=mesh, in_specs=in_specs, out_specs=out_specs, check_vma=False
    )
```

profile of v0, /device:TPU:0, one launch (start us, length us, event | category | flops | bytes accessed | tf_op | source)
XLA Modules:
  0.0 338.7 jit_solution(17743377087618630051)
XLA Ops:
  7.3 1.2 convert_reduce_fusion.1
  8.5 1.2 fusion.54
  9.8 1.5 convolution_convert_fusion.12
  14.2 1.1 fusion.95
  15.5 42.5 %all-reduce.5.cloned.1.call-done = f32[197,768]{1,0:T(8,128)} async-done(((f32[197,768]{1,0:T(8,128)}), f32[197,768]{1,0:T(8,128)}) %all-reduce.5.cloned.1.call-update) | async-done | bytes 605200 | tf_op jit(solution)/shard_map/psum | solution.py:108
  58.0 1.2 fusion.92
  60.4 1.1 convolution_convert_fusion
  61.5 2.1 reshape.284
  63.6 2.4 copy.130
  66.0 4.2 %all-to-all-start = ((bf16[2,2,98,768]{3,1,2,0:T(2,128)(2,1)}), bf16[2,2,98,768]{3,1,2,0:T(2,128)(2,1)}, u32[]{:S(2)}, u32[]{:S(2)}) async-start(bf16[2,2,98,768]{3,1,2,0:T(2,128)(2,1)} %copy.130), calls=%async_computation | async-start | bytes 1204224 | tf_op jit(solution)/shard_map/all_to_all | solution.py:128
  70.7 2.1 fusion.23
  72.8 2.1 reshape.286
  74.9 2.4 copy.134
  77.2 1.5 all-to-all-done
  78.8 4.3 %all-to-all-start.2 = ((bf16[2,2,98,768]{3,1,2,0:T(2,128)(2,1)}), bf16[2,2,98,768]{3,1,2,0:T(2,128)(2,1)}, u32[]{:S(2)}, u32[]{:S(2)}) async-start(bf16[2,2,98,768]{3,1,2,0:T(2,128)(2,1)} %copy.134), calls=%async_computation.2 | async-start | bytes 1204224 | tf_op jit(solution)/shard_map/all_to_all | solution.py:156
  83.1 2.5 fusion.14
  85.6 1.1 copy-done.14
  87.5 1.9 copy.177
  89.5 47.3 %all-reduce.10 = bf16[2,2,98,768]{3,1,2,0:T(2,128)(2,1)} all-reduce(f32[2,2,98,768]{3,1,2,0:T(2,128)} %bitcast.163), channel_id=1, replica_groups=mesh['dp'=4,'expert'=2,'tensor'=4] {'tensor'}, use_global_device_ids=true, to_apply=%region_11.12 | all-reduce | flops 301056 | bytes 1806336 | tf_op jit(solution)/shard_map/psum | solution.py:135
  136.7 4.3 %all-to-all-start.1 = ((bf16[2,2,98,768]{3,1,2,0:T(2,128)(2,1)}), bf16[2,2,98,768]{3,1,2,0:T(2,128)(2,1)}, u32[]{:S(2)}, u32[]{:S(2)}) async-start(bf16[2,2,98,768]{3,1,2,0:T(2,128)(2,1)} %all-reduce.10), calls=%async_computation.1 | async-start | bytes 1204224 | tf_op jit(solution)/shard_map/all_to_all | solution.py:136
  141.1 2.9 fusion.17
  144.0 0.8 copy-done.10
  144.8 1.7 fusion.29
  146.5 1.8 convert_element_type.218
  148.4 2.0 copy.133
  150.3 2.1 reshape.301
  152.4 2.8 multiply_reduce_fusion
  155.3 31.0 %all-reduce.7.cloned.1.call-done = bf16[2,2,98,768]{3,2,0,1:T(8,128)(2,1)} async-done(((bf16[2,2,98,768]{3,2,0,1:T(8,128)(2,1)}), bf16[2,2,98,768]{3,2,0,1:T(8,128)(2,1)}) %all-reduce.7.cloned.1.call-update) | async-done | bytes 602128 | tf_op jit(solution)/shard_map/psum | solution.py:172
  186.3 2.4 copy.136
  188.6 4.2 %all-to-all-start.3 = ((bf16[2,2,98,768]{3,1,2,0:T(2,128)(2,1)}), bf16[2,2,98,768]{3,1,2,0:T(2,128)(2,1)}, u32[]{:S(2)}, u32[]{:S(2)}) async-start(bf16[2,2,98,768]{3,1,2,0:T(2,128)(2,1)} %copy.136), calls=%async_computation.3 | async-start | bytes 1204224 | tf_op jit(solution)/shard_map/all_to_all | solution.py:173
  193.2 1.5 fusion.87
  194.7 6.8 %all-to-all-done.3 = bf16[2,2,98,768]{3,1,2,0:T(2,128)(2,1)} async-done(((bf16[2,2,98,768]{3,1,2,0:T(2,128)(2,1)}), bf16[2,2,98,768]{3,1,2,0:T(2,128)(2,1)}, u32[]{:S(2)}, u32[]{:S(2)}) %all-to-all-start.3) | async-done | bytes 602144 | tf_op jit(solution)/shard_map/all_to_all | solution.py:173
  201.5 2.0 copy.137
  203.5 2.1 reshape.287
  205.6 1.9 multiply_reduce_fusion.2
  207.6 1.1 multiply_add_fusion.1
  209.0 0.9 copy-done.2
  211.7 1.0 fusion.35
  212.7 3.3 bitcast_convert_fusion.1
  216.1 3.8 %bitcast_convert_fusion = bf16[2,768,768]{1,2,0:T(8,128)(2,1)} fusion(bf16[2,2,98,768]{3,1,2,0:T(2,128)(2,1)} %all-to-all-done.2, f32[2,2,98,768]{3,2,0,1:T(8,128)} %copy-done.14), kind=kOutput, calls=%fused_computation | convolution fusion | flops 466311168 | bytes 4165632 | tf_op jit(solution)/shard_map/skcf,skcd->kfd/dot_general | solution.py:163
  220.0 1.0 copy-done.4
  221.0 0.9 convolution_convert_fusion.4
  222.0 2.2 reshape.295
  224.1 1.8 copy.178
  226.0 4.1 %all-to-all-start.6 = ((bf16[8,192,96]{2,1,0:T(8,128)(2,1)}), bf16[8,192,96]{2,1,0:T(8,128)(2,1)}, u32[]{:S(2)}, u32[]{:S(2)}) async-start(bf16[8,192,96]{2,1,0:T(8,128)(2,1)} %bitcast.164), calls=%async_computation.6 | async-start | bytes 786432 | tf_op jit(solution)/shard_map/all_to_all | solution.py:21
  230.1 1.2 convolution_convert_fusion.13
  231.6 6.3 %all-to-all-done.6 = bf16[8,192,96]{2,1,0:T(8,128)(2,1)} async-done(((bf16[8,192,96]{2,1,0:T(8,128)(2,1)}), bf16[8,192,96]{2,1,0:T(8,128)(2,1)}, u32[]{:S(2)}, u32[]{:S(2)}) %all-to-all-start.6) | async-done | bytes 294944 | tf_op jit(solution)/shard_map/all_to_all | solution.py:21
  237.8 1.7 convert_reduce_fusion.3
  239.5 8.2 %all-reduce.9.cloned.1.call-done = bf16[197,768]{1,0:T(8,128)(2,1)} async-done(((bf16[197,768]{1,0:T(8,128)(2,1)}), bf16[197,768]{1,0:T(8,128)(2,1)}) %all-reduce.9.cloned.1.call-update) | async-done | bytes 302608 | tf_op jit(solution)/shard_map/psum | solution.py:238
  247.8 2.0 fusion.56
  249.9 1.0 reduce_sum.244
  251.6 3.6 %all-to-all-start.4 = ((bf16[8,96,8]{1,2,0:T(8,128)(2,1)}), bf16[8,96,8]{1,2,0:T(8,128)(2,1)S(1)}, u32[]{:S(2)}, u32[]{:S(2)}) async-start(bf16[8,96,8]{1,2,0:T(8,128)(2,1)} %concatenate.12), calls=%async_computation.4 | async-start | bytes 32768 | tf_op jit(solution)/shard_map/all_to_all | solution.py:21
  255.2 1.9 copy.164
  257.1 1.4 fusion.38
  258.5 1.3 fusion.37
  260.4 1.1 copy.150
  261.5 4.3 %all-to-all-start.5 = ((bf16[8,3,96,192]{3,2,1,0:T(8,128)(2,1)}), bf16[8,3,96,192]{3,2,1,0:T(8,128)(2,1)}, u32[]{:S(2)}, u32[]{:S(2)}) async-start(bf16[8,3,96,192]{3,2,1,0:T(8,128)(2,1)} %copy.150), calls=%async_computation.5 | async-start | bytes 2359296 | tf_op jit(solution)/shard_map/all_to_all | solution.py:21
  265.8 2.0 fusion.53
  269.0 19.1 %all-to-all-done.5 = bf16[8,3,96,192]{3,2,1,0:T(8,128)(2,1)} async-done(((bf16[8,3,96,192]{3,2,1,0:T(8,128)(2,1)}), bf16[8,3,96,192]{3,2,1,0:T(8,128)(2,1)}, u32[]{:S(2)}, u32[]{:S(2)}) %all-to-all-start.5) | async-done | bytes 884768 | tf_op jit(solution)/shard_map/all_to_all | solution.py:21
  288.0 2.2 convert_reduce_fusion
  290.2 5.2 %reduce-scatter.3.cloned.1.call-done = bf16[2,192,768]{2,1,0:T(8,128)(2,1)} async-done(((bf16[2,768,768]{2,1,0:T(8,128)(2,1)}), bf16[2,192,768]{2,1,0:T(8,128)(2,1)}) %reduce-scatter.3.cloned.1.call-update) | async-done | bytes 589840 | tf_op jit(solution)/shard_map/reduce_scatter | solution.py:181
  295.4 2.2 convert_element_type.252
  297.6 32.4 %reduce-scatter.5.cloned.1.call-done = bf16[2,768,192]{1,2,0:T(8,128)(2,1)} async-done(((bf16[2,768,768]{1,2,0:T(8,128)(2,1)}), bf16[2,768,192]{1,2,0:T(8,128)(2,1)}) %reduce-scatter.5.cloned.1.call-update) | async-done | bytes 589840 | tf_op jit(solution)/shard_map/reduce_scatter | solution.py:184
  330.0 2.2 convert_element_type.254
  (138 shorter events, 10.7 us)
Async XLA Ops:
  7.2 79.5 %copy-start = (bf16[2,768,768]{2,1,0:T(8,128)(2,1)S(1)}, bf16[2,768,768]{2,1,0:T(8,128)(2,1)}, u32[]{:S(2)}) copy-start(bf16[2,768,768]{2,1,0:T(8,128)(2,1)} %param.22) | copy-start | bytes 7077892
  7.2 4.1 %copy-start.6 = (bf16[197,768]{1,0:T(8,128)(2,1)S(1)}, bf16[197,768]{1,0:T(8,128)(2,1)}, u32[]{:S(2)}) copy-start(bf16[197,768]{1,0:T(8,128)(2,1)} %param.13) | copy-start | bytes 907780
  7.2 4.1 %copy-start.17 = (bf16[3,768,192]{1,2,0:T(8,128)(2,1)S(1)}, bf16[3,768,192]{1,2,0:T(8,128)(2,1)}, u32[]{:S(2)}) copy-start(bf16[3,768,192]{1,2,0:T(8,128)(2,1)} %param.16) | copy-start | bytes 2654212
  7.2 50.8 %all-reduce.5.cloned.1.call-start = ((), (), s32[]{:S(2)}) async-start(), calls=%async_computation.9 | async-start | bytes 1228800 | tf_op jit(solution)/shard_map/psum | solution.py:108
  7.3 4.0 %copy-start.34 = (f32[768]{0:T(1024)S(1)}, f32[768]{0:T(1024)}, u32[]{:S(2)}) copy-start(f32[768]{0:T(1024)} %param.14) | copy-start | bytes 9220
  7.3 4.0 %copy-start.39 = (f32[768]{0:T(1024)S(1)}, f32[768]{0:T(1024)}, u32[]{:S(2)}) copy-start(f32[768]{0:T(1024)} %param.15) | copy-start | bytes 9220
  9.7 2.0 copy-start.36
  11.3 1.3 copy-start.24
  11.7 0.9 copy-start.26
  12.1 1.4 copy-start.28
  12.1 2.1 copy-start.15
  12.5 0.9 copy-start.1
  12.6 2.7 copy-start.32
  12.6 2.7 copy-start.33
  13.6 0.6 copy-start.12
  15.3 44.1 %copy-start.31 = (f32[768]{0:T(1024)S(1)}, f32[768]{0:T(1024)}, u32[]{:S(2)}) copy-start(f32[768]{0:T(1024)} %param.18) | copy-start | bytes 9220
  15.3 44.1 %copy-start.38 = (f32[768]{0:T(1024)S(1)}, f32[768]{0:T(1024)}, u32[]{:S(2)}) copy-start(f32[768]{0:T(1024)} %param.19) | copy-start | bytes 9220
  15.5 44.2 %copy-start.30 = (f32[768,4]{0,1:T(4,128)S(1)}, f32[768,4]{0,1:T(4,128)}, u32[]{:S(2)}) copy-start(f32[768,4]{0,1:T(4,128)} %param.20) | copy-start | bytes 36868
  59.7 0.7 copy-start.8
  66.0 12.8 %all-to-all-start = ((bf16[2,2,98,768]{3,1,2,0:T(2,128)(2,1)}), bf16[2,2,98,768]{3,1,2,0:T(2,128)(2,1)}, u32[]{:S(2)}, u32[]{:S(2)}) async-start(bf16[2,2,98,768]{3,1,2,0:T(2,128)(2,1)} %copy.130), calls=%async_computation | async-start | bytes 1204224 | tf_op jit(solution)/shard_map/all_to_all | solution.py:128
  78.8 58.0 %all-to-all-start.2 = ((bf16[2,2,98,768]{3,1,2,0:T(2,128)(2,1)}), bf16[2,2,98,768]{3,1,2,0:T(2,128)(2,1)}, u32[]{:S(2)}, u32[]{:S(2)}) async-start(bf16[2,2,98,768]{3,1,2,0:T(2,128)(2,1)} %copy.134), calls=%async_computation.2 | async-start | bytes 1204224 | tf_op jit(solution)/shard_map/all_to_all | solution.py:156
  85.6 1.1 copy-start.14
  136.7 11.6 %all-to-all-start.1 = ((bf16[2,2,98,768]{3,1,2,0:T(2,128)(2,1)}), bf16[2,2,98,768]{3,1,2,0:T(2,128)(2,1)}, u32[]{:S(2)}, u32[]{:S(2)}) async-start(bf16[2,2,98,768]{3,1,2,0:T(2,128)(2,1)} %all-reduce.10), calls=%async_computation.1 | async-start | bytes 1204224 | tf_op jit(solution)/shard_map/all_to_all | solution.py:136
  141.0 45.3 %all-reduce.7.cloned.1.call-start = ((), (), s32[]{:S(2)}) async-start(), calls=%async_computation.10 | async-start | bytes 1277952 | tf_op jit(solution)/shard_map/psum | solution.py:172
  141.1 3.7 %copy-start.5 = (bf16[2,768,768]{2,1,0:T(8,128)(2,1)S(1)}, bf16[2,768,768]{2,1,0:T(8,128)(2,1)}, u32[]{:S(2)}) copy-start(bf16[2,768,768]{2,1,0:T(8,128)(2,1)} %param.21) | copy-start | bytes 7077892
  144.0 0.8 copy-start.10
  188.6 12.9 %all-to-all-start.3 = ((bf16[2,2,98,768]{3,1,2,0:T(2,128)(2,1)}), bf16[2,2,98,768]{3,1,2,0:T(2,128)(2,1)}, u32[]{:S(2)}, u32[]{:S(2)}) async-start(bf16[2,2,98,768]{3,1,2,0:T(2,128)(2,1)} %copy.136), calls=%async_computation.3 | async-start | bytes 1204224 | tf_op jit(solution)/shard_map/all_to_all | solution.py:173
  192.9 54.9 %all-reduce.9.cloned.1.call-start = ((), (), s32[]{:S(2)}) async-start(), calls=%async_computation.11 | async-start | bytes 614400 | tf_op jit(solution)/shard_map/psum | solution.py:238
  205.6 2.0 copy-start.9
  205.6 2.0 copy-start.23
  207.5 1.1 copy-start.16
  207.5 1.4 copy-start.13
  208.6 1.8 copy-start.3
  208.6 1.3 copy-start.2
  208.6 1.3 copy-start.25
  208.6 1.6 copy-start.29
  208.6 1.8 copy-start.27
  209.9 1.2 copy-start.18
  210.4 1.2 copy-start.21
  210.7 1.0 copy-start.19
  211.4 1.4 copy-start.11
  212.7 82.8 %reduce-scatter.3.cloned.1.call-start = ((), (), s32[]{:S(2)}) async-start(), calls=%async_computation.12 | async-start | bytes 2949120 | tf_op jit(solution)/shard_map/reduce_scatter | solution.py:181
  216.1 113.9 %reduce-scatter.5.cloned.1.call-start = ((), (), s32[]{:S(2)}) async-start(), calls=%async_computation.13 | async-start | bytes 2949120 | tf_op jit(solution)/shard_map/reduce_scatter | solution.py:184
  219.9 1.1 copy-start.4
  224.1 23.6 %copy-start.35 = (f32[768]{0:T(1024)S(1)}, f32[768]{0:T(1024)}, u32[]{:S(2)}) copy-start(f32[768]{0:T(1024)} %param.14) | copy-start | bytes 9220
  224.1 23.6 %copy-start.37 = (f32[197]{0:T(256)S(1)}, f32[197]{0:T(256)}, u32[]{:S(2)}) copy-start(f32[197]{0:T(256)} %copy-done.36) | copy-start | bytes 2368
  224.1 23.6 %copy-start.40 = (f32[768]{0:T(1024)S(1)}, f32[768]{0:T(1024)}, u32[]{:S(2)}) copy-start(f32[768]{0:T(1024)} %param.15) | copy-start | bytes 9220
  226.0 11.9 %all-to-all-start.6 = ((bf16[8,192,96]{2,1,0:T(8,128)(2,1)}), bf16[8,192,96]{2,1,0:T(8,128)(2,1)}, u32[]{:S(2)}, u32[]{:S(2)}) async-start(bf16[8,192,96]{2,1,0:T(8,128)(2,1)} %bitcast.164), calls=%async_computation.6 | async-start | bytes 786432 | tf_op jit(solution)/shard_map/all_to_all | solution.py:21
  239.5 18.9 %copy-start.20 = (bf16[3,64,197]{2,1,0:T(8,128)(2,1)S(1)}, bf16[3,64,197]{2,1,0:T(8,128)(2,1)}, u32[]{:S(2)}) copy-start(bf16[3,64,197]{2,1,0:T(8,128)(2,1)} %copy-done.19) | copy-start | bytes 226948
  251.6 9.9 %all-to-all-start.4 = ((bf16[8,96,8]{1,2,0:T(8,128)(2,1)}), bf16[8,96,8]{1,2,0:T(8,128)(2,1)S(1)}, u32[]{:S(2)}, u32[]{:S(2)}) async-start(bf16[8,96,8]{1,2,0:T(8,128)(2,1)} %concatenate.12), calls=%async_computation.4 | async-start | bytes 32768 | tf_op jit(solution)/shard_map/all_to_all | solution.py:21
  257.1 2.7 copy-start.7
  257.1 2.7 copy-start.22
  261.5 26.5 %all-to-all-start.5 = ((bf16[8,3,96,192]{3,2,1,0:T(8,128)(2,1)}), bf16[8,3,96,192]{3,2,1,0:T(8,128)(2,1)}, u32[]{:S(2)}, u32[]{:S(2)}) async-start(bf16[8,3,96,192]{3,2,1,0:T(8,128)(2,1)} %copy.150), calls=%async_computation.5 | async-start | bytes 2359296 | tf_op jit(solution)/shard_map/all_to_all | solution.py:21
Sparse Core Ops, SparseCore 0:
  15.4 42.5 all-reduce.4
  146.6 39.5 all-reduce.6
  212.8 34.9 all-reduce.8
  250.1 45.2 reduce-scatter.2
  297.8 32.1 reduce-scatter.4
where the time goes:
time: 341 us; the launch traced here: 339 us
  waiting for transfers between devices  153 us (45%)
  blocking collectives  47.3 us (14%)
  matrix products  37.3 us (11%)
  local copies, waits for them, and re-layouts  36.2 us (11%)
  starting transfers between devices  29.3 us (9%)
  other arithmetic  21 us (6%)
  between operations  14.5 us (4%)
    psum x1, blocking collectives, per_device(): summed = lax.psum(partial_value, 'tensor')  47.3 us
    psum x1, waiting for transfers between devices, per_device(): attended = lax.psum(partial_attn, 'tensor')  42.5 us
    reduce_scatter x1, waiting for transfers between devices, per_device(): lax.psum_scatter(local_out_grad.astype(jnp.bfloat16), 'dp', scatter_dimen...  32.4 us
    psum x1, waiting for transfers between devices, per_device(): back_sum = lax.psum(partial_back.astype(jnp.bfloat16), 'tensor')  31 us
    all_to_all x3, waiting for transfers between devices, sent_and_summed(): lax.all_to_all(cut_along(shard, dim, devices), axis, 0, 0, tiled=True)  25.3 us
    all_to_all x3, starting transfers between devices, sent_and_summed(): lax.all_to_all(cut_along(shard, dim, devices), axis, 0, 0, tiled=True)  11.9 us
    psum x1, waiting for transfers between devices, per_device(): lax.psum(partial_first.astype(jnp.bfloat16), 'tensor').astype(jnp.float32)  8.2 us
    all_to_all x1, waiting for transfers between devices, per_device(): lax.all_to_all(back_sum, 'expert', split_axis=0, concat_axis=0, tiled=True)  6.82 us
  transfers between devices with their start and end apart: 12, of which 9 were waited for; matrix products, arithmetic and copies ran while one was open for 18% of the time, Pallas kernels for 0%

commit v1 on v0

--- a/solution.py
+++ b/solution.py
@@ -169,7 +169,9 @@
     partial_back = jnp.einsum(
         "skcf,kdf->skcd", pre_grad, expert_in, preferred_element_type=jnp.float32
     )
-    back_sum = lax.psum(partial_back.astype(jnp.bfloat16), "tensor")
+    x = partial_back.astype(jnp.bfloat16)
+    terms = lax.all_gather(x, "tensor", axis=0, tiled=False)
+    back_sum = terms.sum(axis=0)
     back_home = lax.all_to_all(back_sum, "expert", split_axis=0, concat_axis=0, tiled=True)
     back_rows = jnp.einsum(
         "rjq,qd->rd",

time: 341 us -> 365 us (1.070)
  blocking collectives: 47.3 us -> 86.1 us
  waiting for transfers between devices: 153 us -> 132 us
  matrix products: 37.3 us -> 41.2 us
    psum x1, blocking collectives: 47.3 us -> 86.1 us  [per_device(): summed = lax.psum(partial_value, 'tensor')]
    psum x1 -> x0, waiting for transfers between devices: 31 us -> none  [per_device(): back_sum = lax.psum(partial_back.astype(jnp.bfloat16), 'tensor')]
    reduce_scatter x1, waiting for transfers between devices: 5.22 us -> 26.5 us  [per_device(): lax.psum_scatter(local_in_grad.astype(jnp.bfloat16), 'dp', scatter_dimens...]
    all_to_all x3, waiting for transfers between devices: 25.3 us -> 6.45 us  [sent_and_summed(): lax.all_to_all(cut_along(shard, dim, devices), axis, 0, 0, tiled=True)]
    all_to_all x1, waiting for transfers between devices: 0.01 us -> 5.6 us  [per_device(): lax.all_to_all(grad_send, 'expert', split_axis=0, concat_axis=0, tiled=True)]
    all_to_all x1, waiting for transfers between devices: 0.01 us -> 5.43 us  [per_device(): lax.all_to_all(summed.astype(jnp.bfloat16), 'expert', split_axis=0, conca...]
  transfers between devices with their start and end apart: 12 -> 12, of which waited for: 9 -> 10; matrix products, arithmetic and copies ran while one was open for 18% -> 16% of each run, Pallas kernels for 0% -> 0%
where the time goes in v1:
time: 365 us; the launch traced here: 363 us
  waiting for transfers between devices  132 us (36%)
  blocking collectives  86.1 us (24%)
  matrix products  41.2 us (11%)
  local copies, waits for them, and re-layouts  35.9 us (10%)
  starting transfers between devices  29.3 us (8%)
  other arithmetic  24.1 us (7%)
  between operations  14.5 us (4%)
    psum x1, blocking collectives, per_device(): summed = lax.psum(partial_value, 'tensor')  86.1 us
    psum x1, waiting for transfers between devices, per_device(): attended = lax.psum(partial_attn, 'tensor')  42.5 us
    reduce_scatter x1, waiting for transfers between devices, per_device(): lax.psum_scatter(local_out_grad.astype(jnp.bfloat16), 'dp', scatter_dimen...  32.3 us
    reduce_scatter x1, waiting for transfers between devices, per_device(): lax.psum_scatter(local_in_grad.astype(jnp.bfloat16), 'dp', scatter_dimens...  26.5 us
    all_to_all x3, starting transfers between devices, sent_and_summed(): lax.all_to_all(cut_along(shard, dim, devices), axis, 0, 0, tiled=True)  11.9 us
    psum x1, waiting for transfers between devices, per_device(): lax.psum(partial_first.astype(jnp.bfloat16), 'tensor').astype(jnp.float32)  7.69 us
  transfers between devices with their start and end apart: 12, of which 10 were waited for; matrix products, arithmetic and copies ran while one was open for 16% of the time, Pallas kernels for 0%

profile of v1, /device:TPU:0, one launch (start us, length us, event | category | flops | bytes accessed | tf_op | source)
XLA Modules:
  0.0 363.1 jit_solution(13094152830921790469)
XLA Ops:
  7.3 1.2 convert_reduce_fusion.1
  8.5 1.2 fusion.54
  9.8 1.5 convolution_convert_fusion.11
  14.2 1.1 fusion.95
  15.5 42.5 %all-reduce.4.cloned.1.call-done = f32[197,768]{1,0:T(8,128)} async-done(((f32[197,768]{1,0:T(8,128)}), f32[197,768]{1,0:T(8,128)}) %all-reduce.4.cloned.1.call-update) | async-done | bytes 605200 | tf_op jit(solution)/shard_map/psum | solution.py:108
  58.0 1.2 fusion.92
  60.3 1.1 convolution_convert_fusion
  61.5 2.1 reshape.284
  63.6 2.4 copy.129
  65.9 4.2 %all-to-all-start = ((bf16[2,2,98,768]{3,1,2,0:T(2,128)(2,1)}), bf16[2,2,98,768]{3,1,2,0:T(2,128)(2,1)}, u32[]{:S(2)}, u32[]{:S(2)}) async-start(bf16[2,2,98,768]{3,1,2,0:T(2,128)(2,1)} %copy.129), calls=%async_computation | async-start | bytes 1204224 | tf_op jit(solution)/shard_map/all_to_all | solution.py:128
  70.2 1.4 fusion.94
  72.1 2.1 fusion.23
  74.2 2.1 reshape.286
  76.3 2.4 copy.133
  78.7 4.2 %all-to-all-start.2 = ((bf16[2,2,98,768]{3,1,2,0:T(2,128)(2,1)}), bf16[2,2,98,768]{3,1,2,0:T(2,128)(2,1)}, u32[]{:S(2)}, u32[]{:S(2)}) async-start(bf16[2,2,98,768]{3,1,2,0:T(2,128)(2,1)} %copy.133), calls=%async_computation.2 | async-start | bytes 1204224 | tf_op jit(solution)/shard_map/all_to_all | solution.py:156
  83.0 2.8 fusion.14
  85.8 5.6 %all-to-all-done.2 = bf16[2,2,98,768]{3,1,2,0:T(2,128)(2,1)} async-done(((bf16[2,2,98,768]{3,1,2,0:T(2,128)(2,1)}), bf16[2,2,98,768]{3,1,2,0:T(2,128)(2,1)}, u32[]{:S(2)}, u32[]{:S(2)}) %all-to-all-start.2) | async-done | bytes 602144 | tf_op jit(solution)/shard_map/all_to_all | solution.py:156
  91.4 3.4 fusion.17
  95.7 1.7 fusion.29
  97.5 2.8 fusion.6
  100.3 2.0 copy.176
  102.3 86.1 %all-reduce.7 = bf16[2,2,98,768]{3,1,2,0:T(2,128)(2,1)} all-reduce(f32[2,2,98,768]{3,1,2,0:T(2,128)} %bitcast.164), channel_id=1, replica_groups=mesh['dp'=4,'expert'=2,'tensor'=4] {'tensor'}, use_global_device_ids=true, to_apply=%region_11.12 | all-reduce | flops 301056 | bytes 1806336 | tf_op jit(solution)/shard_map/psum | solution.py:135
  188.4 4.4 %all-to-all-start.1 = ((bf16[2,2,98,768]{3,1,2,0:T(2,128)(2,1)}), bf16[2,2,98,768]{3,1,2,0:T(2,128)(2,1)}, u32[]{:S(2)}, u32[]{:S(2)}) async-start(bf16[2,2,98,768]{3,1,2,0:T(2,128)(2,1)} %all-reduce.7), calls=%async_computation.1 | async-start | bytes 1204224 | tf_op jit(solution)/shard_map/all_to_all | solution.py:136
  192.8 1.8 convert_element_type.220
  194.6 5.4 %all-to-all-done.1 = bf16[2,2,98,768]{3,1,2,0:T(2,128)(2,1)} async-done(((bf16[2,2,98,768]{3,1,2,0:T(2,128)(2,1)}), bf16[2,2,98,768]{3,1,2,0:T(2,128)(2,1)}, u32[]{:S(2)}, u32[]{:S(2)}) %all-to-all-start.1) | async-done | bytes 602144 | tf_op jit(solution)/shard_map/all_to_all | solution.py:136
  200.1 2.0 copy.132
  202.0 2.1 reshape.302
  204.1 2.8 multiply_reduce_fusion
  207.0 3.1 reduce_sum.246
  210.1 2.4 copy.135
  212.5 4.2 %all-to-all-start.3 = ((bf16[2,2,98,768]{3,1,2,0:T(2,128)(2,1)}), bf16[2,2,98,768]{3,1,2,0:T(2,128)(2,1)}, u32[]{:S(2)}, u32[]{:S(2)}) async-start(bf16[2,2,98,768]{3,1,2,0:T(2,128)(2,1)} %copy.135), calls=%async_computation.3 | async-start | bytes 1204224 | tf_op jit(solution)/shard_map/all_to_all | solution.py:175
  216.8 1.5 fusion.87
  218.3 5.5 %all-to-all-done.3 = bf16[2,2,98,768]{3,1,2,0:T(2,128)(2,1)} async-done(((bf16[2,2,98,768]{3,1,2,0:T(2,128)(2,1)}), bf16[2,2,98,768]{3,1,2,0:T(2,128)(2,1)}, u32[]{:S(2)}, u32[]{:S(2)}) %all-to-all-start.3) | async-done | bytes 602144 | tf_op jit(solution)/shard_map/all_to_all | solution.py:175
  223.8 2.0 copy.136
  225.8 2.1 reshape.287
  227.8 1.9 multiply_reduce_fusion.2
  229.8 1.1 multiply_add_fusion.1
  231.2 1.0 copy-done.2
  234.2 1.0 fusion.35
  235.3 3.3 bitcast_convert_fusion.1
  238.7 3.8 %bitcast_convert_fusion = bf16[2,768,768]{1,2,0:T(8,128)(2,1)} fusion(bf16[2,2,98,768]{3,1,2,0:T(2,128)(2,1)} %all-to-all-done.2, f32[2,2,98,768]{3,2,0,1:T(8,128)} %fusion.14), kind=kOutput, calls=%fused_computation | convolution fusion | flops 466311168 | bytes 4165632 | tf_op jit(solution)/shard_map/skcf,skcd->kfd/dot_general | solution.py:163
  242.5 1.0 copy-done.4
  243.6 1.0 convolution_convert_fusion.4
  244.5 2.2 reshape.295
  246.7 1.8 copy.177
  248.5 4.1 %all-to-all-start.6 = ((bf16[8,192,96]{2,1,0:T(8,128)(2,1)}), bf16[8,192,96]{2,1,0:T(8,128)(2,1)}, u32[]{:S(2)}, u32[]{:S(2)}) async-start(bf16[8,192,96]{2,1,0:T(8,128)(2,1)} %bitcast.166), calls=%async_computation.6 | async-start | bytes 786432 | tf_op jit(solution)/shard_map/all_to_all | solution.py:21
  252.6 1.2 convolution_convert_fusion.13
  254.1 6.3 %all-to-all-done.6 = bf16[8,192,96]{2,1,0:T(8,128)(2,1)} async-done(((bf16[8,192,96]{2,1,0:T(8,128)(2,1)}), bf16[8,192,96]{2,1,0:T(8,128)(2,1)}, u32[]{:S(2)}, u32[]{:S(2)}) %all-to-all-start.6) | async-done | bytes 294944 | tf_op jit(solution)/shard_map/all_to_all | solution.py:21
  260.4 1.7 convert_reduce_fusion.3
  262.1 7.7 %all-reduce.6.cloned.1.call-done = bf16[197,768]{1,0:T(8,128)(2,1)} async-done(((bf16[197,768]{1,0:T(8,128)(2,1)}), bf16[197,768]{1,0:T(8,128)(2,1)}) %all-reduce.6.cloned.1.call-update) | async-done | bytes 302608 | tf_op jit(solution)/shard_map/psum | solution.py:240
  269.8 2.0 fusion.56
  271.8 1.9 copy.163
  273.8 1.0 reduce_sum.257
  275.5 3.6 all-to-all-start.4
  279.1 1.4 fusion.36
  280.5 1.3 fusion.37
  282.4 1.2 copy.149
  283.8 4.3 %all-to-all-start.5 = ((bf16[8,3,96,192]{3,2,1,0:T(8,128)(2,1)}), bf16[8,3,96,192]{3,2,1,0:T(8,128)(2,1)}, u32[]{:S(2)}, u32[]{:S(2)}) async-start(bf16[8,3,96,192]{3,2,1,0:T(8,128)(2,1)} %copy.149), calls=%async_computation.5 | async-start | bytes 2359296 | tf_op jit(solution)/shard_map/all_to_all | solution.py:21
  288.1 2.1 fusion.53
  291.3 26.5 %reduce-scatter.3.cloned.1.call-done = bf16[2,192,768]{2,1,0:T(8,128)(2,1)} async-done(((bf16[2,768,768]{2,1,0:T(8,128)(2,1)}), bf16[2,192,768]{2,1,0:T(8,128)(2,1)}) %reduce-scatter.3.cloned.1.call-update) | async-done | bytes 589840 | tf_op jit(solution)/shard_map/reduce_scatter | solution.py:183
  317.7 2.2 convert_element_type.254
  319.9 32.3 %reduce-scatter.5.cloned.1.call-done = bf16[2,768,192]{1,2,0:T(8,128)(2,1)} async-done(((bf16[2,768,768]{1,2,0:T(8,128)(2,1)}), bf16[2,768,192]{1,2,0:T(8,128)(2,1)}) %reduce-scatter.5.cloned.1.call-update) | async-done | bytes 589840 | tf_op jit(solution)/shard_map/reduce_scatter | solution.py:186
  352.2 2.2 convert_element_type.256
  354.4 2.2 convert_reduce_fusion
  (133 shorter events, 11.1 us)
Async XLA Ops:
  7.2 75.8 %copy-start = (bf16[2,768,768]{2,1,0:T(8,128)(2,1)S(1)}, bf16[2,768,768]{2,1,0:T(8,128)(2,1)}, u32[]{:S(2)}) copy-start(bf16[2,768,768]{2,1,0:T(8,128)(2,1)} %param.21) | copy-start | bytes 7077892
  7.2 4.1 %copy-start.5 = (bf16[197,768]{1,0:T(8,128)(2,1)S(1)}, bf16[197,768]{1,0:T(8,128)(2,1)}, u32[]{:S(2)}) copy-start(bf16[197,768]{1,0:T(8,128)(2,1)} %param.13) | copy-start | bytes 907780
  7.2 4.1 %copy-start.15 = (bf16[3,768,192]{1,2,0:T(8,128)(2,1)S(1)}, bf16[3,768,192]{1,2,0:T(8,128)(2,1)}, u32[]{:S(2)}) copy-start(bf16[3,768,192]{1,2,0:T(8,128)(2,1)} %param.16) | copy-start | bytes 2654212
  7.2 50.8 %all-reduce.4.cloned.1.call-start = ((), (), s32[]{:S(2)}) async-start(), calls=%async_computation.9 | async-start | bytes 1228800 | tf_op jit(solution)/shard_map/psum | solution.py:108
  7.3 4.0 %copy-start.31 = (f32[768]{0:T(1024)S(1)}, f32[768]{0:T(1024)}, u32[]{:S(2)}) copy-start(f32[768]{0:T(1024)} %param.14) | copy-start | bytes 9220
  7.3 4.0 %copy-start.36 = (f32[768]{0:T(1024)S(1)}, f32[768]{0:T(1024)}, u32[]{:S(2)}) copy-start(f32[768]{0:T(1024)} %param.15) | copy-start | bytes 9220
  9.7 2.0 copy-start.33
  11.3 0.9 copy-start.23
  11.7 0.9 copy-start.25
  12.1 1.4 copy-start.21
  12.1 2.0 copy-start.13
  12.5 0.8 copy-start.1
  12.6 2.7 copy-start.29
  12.6 2.7 copy-start.30
  13.5 0.6 copy-start.11
  15.3 44.1 %copy-start.28 = (f32[768]{0:T(1024)S(1)}, f32[768]{0:T(1024)}, u32[]{:S(2)}) copy-start(f32[768]{0:T(1024)} %param.18) | copy-start | bytes 9220
  15.3 44.1 %copy-start.35 = (f32[768]{0:T(1024)S(1)}, f32[768]{0:T(1024)}, u32[]{:S(2)}) copy-start(f32[768]{0:T(1024)} %param.19) | copy-start | bytes 9220
  59.6 0.7 copy-start.7
  63.5 6.6 %copy-start.27 = (f32[768,4]{0,1:T(4,128)S(1)}, f32[768,4]{0,1:T(4,128)}, u32[]{:S(2)}) copy-start(f32[768,4]{0,1:T(4,128)} %param.20) | copy-start | bytes 36868
  65.9 12.8 %all-to-all-start = ((bf16[2,2,98,768]{3,1,2,0:T(2,128)(2,1)}), bf16[2,2,98,768]{3,1,2,0:T(2,128)(2,1)}, u32[]{:S(2)}, u32[]{:S(2)}) async-start(bf16[2,2,98,768]{3,1,2,0:T(2,128)(2,1)} %copy.129), calls=%async_computation | async-start | bytes 1204224 | tf_op jit(solution)/shard_map/all_to_all | solution.py:128
  78.7 12.7 %all-to-all-start.2 = ((bf16[2,2,98,768]{3,1,2,0:T(2,128)(2,1)}), bf16[2,2,98,768]{3,1,2,0:T(2,128)(2,1)}, u32[]{:S(2)}, u32[]{:S(2)}) async-start(bf16[2,2,98,768]{3,1,2,0:T(2,128)(2,1)} %copy.133), calls=%async_computation.2 | async-start | bytes 1204224 | tf_op jit(solution)/shard_map/all_to_all | solution.py:156
  83.0 124.0 %all-gather.3.cloned.1.call-start = ((), (), s32[]{:S(2)}) async-start(), calls=%async_computation.13 | async-start | bytes 3194880 | tf_op jit(solution)/shard_map/all_gather | solution.py:173
  94.9 0.8 copy-start.9
  188.4 11.7 %all-to-all-start.1 = ((bf16[2,2,98,768]{3,1,2,0:T(2,128)(2,1)}), bf16[2,2,98,768]{3,1,2,0:T(2,128)(2,1)}, u32[]{:S(2)}, u32[]{:S(2)}) async-start(bf16[2,2,98,768]{3,1,2,0:T(2,128)(2,1)} %all-reduce.7), calls=%async_computation.1 | async-start | bytes 1204224 | tf_op jit(solution)/shard_map/all_to_all | solution.py:136
  212.5 11.3 %all-to-all-start.3 = ((bf16[2,2,98,768]{3,1,2,0:T(2,128)(2,1)}), bf16[2,2,98,768]{3,1,2,0:T(2,128)(2,1)}, u32[]{:S(2)}, u32[]{:S(2)}) async-start(bf16[2,2,98,768]{3,1,2,0:T(2,128)(2,1)} %copy.135), calls=%async_computation.3 | async-start | bytes 1204224 | tf_op jit(solution)/shard_map/all_to_all | solution.py:175
  216.7 53.1 %all-reduce.6.cloned.1.call-start = ((), (), s32[]{:S(2)}) async-start(), calls=%async_computation.10 | async-start | bytes 614400 | tf_op jit(solution)/shard_map/psum | solution.py:240
  227.8 2.0 copy-start.8
  227.8 2.0 copy-start.20
  229.8 1.1 copy-start.14
  230.9 1.9 copy-start.3
  230.9 1.3 copy-start.2
  230.9 1.6 copy-start.12
  230.9 1.6 copy-start.22
  231.2 1.7 copy-start.26
  232.2 0.9 copy-start.24
  232.4 1.2 copy-start.16
  233.1 0.8 copy-start.19
  233.3 0.9 copy-start.17
  233.9 1.4 copy-start.10
  235.2 82.5 %reduce-scatter.3.cloned.1.call-start = ((), (), s32[]{:S(2)}) async-start(), calls=%async_computation.11 | async-start | bytes 2949120 | tf_op jit(solution)/shard_map/reduce_scatter | solution.py:183
  238.6 113.6 %reduce-scatter.5.cloned.1.call-start = ((), (), s32[]{:S(2)}) async-start(), calls=%async_computation.12 | async-start | bytes 2949120 | tf_op jit(solution)/shard_map/reduce_scatter | solution.py:186
  242.5 1.1 copy-start.4
  246.7 23.1 %copy-start.32 = (f32[768]{0:T(1024)S(1)}, f32[768]{0:T(1024)}, u32[]{:S(2)}) copy-start(f32[768]{0:T(1024)} %param.14) | copy-start | bytes 9220
  246.7 23.1 %copy-start.34 = (f32[197]{0:T(256)S(1)}, f32[197]{0:T(256)}, u32[]{:S(2)}) copy-start(f32[197]{0:T(256)} %copy-done.33) | copy-start | bytes 2368
  246.7 23.1 %copy-start.37 = (f32[768]{0:T(1024)S(1)}, f32[768]{0:T(1024)}, u32[]{:S(2)}) copy-start(f32[768]{0:T(1024)} %param.15) | copy-start | bytes 9220
  248.5 11.9 %all-to-all-start.6 = ((bf16[8,192,96]{2,1,0:T(8,128)(2,1)}), bf16[8,192,96]{2,1,0:T(8,128)(2,1)}, u32[]{:S(2)}, u32[]{:S(2)}) async-start(bf16[8,192,96]{2,1,0:T(8,128)(2,1)} %bitcast.166), calls=%async_computation.6 | async-start | bytes 786432 | tf_op jit(solution)/shard_map/all_to_all | solution.py:21
  262.1 18.4 %copy-start.18 = (bf16[3,64,197]{2,1,0:T(8,128)(2,1)S(1)}, bf16[3,64,197]{2,1,0:T(8,128)(2,1)}, u32[]{:S(2)}) copy-start(bf16[3,64,197]{2,1,0:T(8,128)(2,1)} %copy-done.17) | copy-start | bytes 226948
  275.5 8.3 %all-to-all-start.4 = ((bf16[8,96,8]{1,2,0:T(8,128)(2,1)}), bf16[8,96,8]{1,2,0:T(8,128)(2,1)S(1)}, u32[]{:S(2)}, u32[]{:S(2)}) async-start(bf16[8,96,8]{1,2,0:T(8,128)(2,1)} %concatenate.12), calls=%async_computation.4 | async-start | bytes 32768 | tf_op jit(solution)/shard_map/all_to_all | solution.py:21
  279.1 2.7 copy-start.6
  283.8 70.6 %all-to-all-start.5 = ((bf16[8,3,96,192]{3,2,1,0:T(8,128)(2,1)}), bf16[8,3,96,192]{3,2,1,0:T(8,128)(2,1)}, u32[]{:S(2)}, u32[]{:S(2)}) async-start(bf16[8,3,96,192]{3,2,1,0:T(8,128)(2,1)} %copy.149), calls=%async_computation.5 | async-start | bytes 2359296 | tf_op jit(solution)/shard_map/all_to_all | solution.py:21
Sparse Core Ops, SparseCore 0:
  15.4 42.5 all-reduce.3
  97.6 88.5 all-gather.2
  235.3 34.4 all-reduce.5
  272.2 45.5 reduce-scatter.2
  320.1 32.0 reduce-scatter.4
